TPU v7x, 512 devices: a whole 4x4x16 slice. The times are simulated.
512 devices in a mesh: row: 8 (over y, core), col: 16 (over z), ch: 4 (over x).
Axes of the slice: x: 4, y: 4, z: 16, core: 2. Of those that a mesh axis runs over, the one named last changes fastest.
Arguments:
- image: bfloat16 [256, 32, 2048], P('ch', 'row', 'col'), may hold values from -6 to 6
- depth_kernel: float32 [256, 49], P('ch'), may hold values from -0.875 to 0.875
- norm_gain: float32 [256], P('ch'), may hold values from 0.25 to 1.75
- norm_shift: float32 [256], P('ch'), may hold values from -3 to 3
- expand_weight: bfloat16 [256, 1024], P(None, 'ch'), may hold values from -0.375 to 0.375
- expand_bias: float32 [1024], replicated, may hold values from -3 to 3
- reduce_weight: bfloat16 [1024, 256], P('ch'), may hold values from -0.1875 to 0.1875
- cotangent: bfloat16 [256, 32, 2048], P('ch', 'row', 'col'), may hold values from -6 to 6
Outputs:
- result: bfloat16 [256, 32, 2048], P('ch', 'row', 'col')
- grad_image: bfloat16 [256, 32, 2048], P('ch', 'row', 'col')
- grad_kernel: float32 [256, 49], P('ch')
- grad_gain: float32 [256], P('ch')
- grad_shift: float32 [256], P('ch')
- grad_expand: float32 [256, 1024], P(None, 'ch')
- grad_offset: float32 [1024], P('ch')
- grad_reduce: float32 [1024, 256], P('ch')
All inputs are finite; a program needn't handle non-finite values.
Results may differ from a plain program's by a relative error of at most 0.011.
Values may be sent and summed in bfloat16 or wider, within the bound.
No kernel may reach another device: no remote copies, remote signals or barrier semaphores. Data moves between devices by JAX's collectives and lax.ppermute only.
A program may use at most 64 MiB of HBM per device.

v0:
```python
import jax
import jax.numpy as jnp
from jax import lax
from jax.sharding import PartitionSpec as P

KSIZE = 7
epsilon = 1e-06
root_two_pi = 0.7978845608028654
cubic_coef = 0.044715


def padded_2(x, sides, width):
    for axis, dim in sides:
        size, length = (lax.axis_size(axis), x.shape[dim])
        up = [(i, (i + 1) % size) for i in range(size - 1)]
        down = [(j, i) for i, j in up]
        last = lax.slice_in_dim(x, length - width, length, axis=dim)
        leading = lax.slice_in_dim(x, 0, width, axis=dim)
        before = lax.ppermute(last, axis, up)
        after = lax.ppermute(leading, axis, down)
        x = jnp.concatenate([before, x, after], axis=dim)
    return x


def product(left, right, dims):
    return lax.dot_general(
        left.astype(jnp.float32),
        right.astype(jnp.float32),
        dims,
        preferred_element_type=jnp.float32,
    )


def gelu_pair(hidden):
    inner = root_two_pi * (hidden + cubic_coef * hidden * hidden * hidden)
    tangent = jnp.tanh(inner)
    value = 0.5 * hidden * (1.0 + tangent)
    slope = 0.5 * (1.0 + tangent) + 0.5 * hidden * (1.0 - tangent * tangent) * root_two_pi * (
        1.0 + 3.0 * cubic_coef * hidden * hidden
    )
    return (value, slope)


def tap_window(padded, kernel, tap, first, second, tile_rows, tile_cols):
    window = lax.dynamic_slice(
        padded, (jnp.int32(0), first, second), (padded.shape[0], tile_rows, tile_cols)
    )
    weight = lax.dynamic_slice_in_dim(kernel, tap, 1, 1)
    return weight[:, :, None] * window


def forward_taps(padded, kernel, span, tile_rows, tile_cols):

    def forward_step(tap, accum):
        tap = jnp.asarray(tap).astype(jnp.int32)
        first = tap // span
        second = tap % span
        return accum + tap_window(padded, kernel, tap, first, second, tile_rows, tile_cols)

    accum = jnp.zeros((padded.shape[0], tile_rows, tile_cols), jnp.float32)
    return lax.fori_loop(0, span * span, forward_step, accum)


def backward_taps(padded, kernel, span, tile_rows, tile_cols):
    reach = span - 1

    def backward_step(tap, accum):
        tap = jnp.asarray(tap).astype(jnp.int32)
        first = reach - tap // span
        second = reach - tap % span
        return accum + tap_window(padded, kernel, tap, first, second, tile_rows, tile_cols)

    accum = jnp.zeros((padded.shape[0], tile_rows, tile_cols), jnp.float32)
    return lax.fori_loop(0, span * span, backward_step, accum)


def kernel_grad(grad_mixed, padded, span, tile_rows, tile_cols):

    def kernel_step(tap, table):
        tap = jnp.asarray(tap).astype(jnp.int32)
        first = tap // span
        second = tap % span
        window = lax.dynamic_slice(
            padded, (jnp.int32(0), first, second), (padded.shape[0], tile_rows, tile_cols)
        )
        column = jnp.sum(grad_mixed * window, axis=(1, 2))
        return lax.dynamic_update_slice_in_dim(table, column[:, None], tap, 1)

    table = jnp.zeros((grad_mixed.shape[0], span * span), jnp.float32)
    return lax.fori_loop(0, span * span, kernel_step, table)


def body(
    image, depth_kernel, norm_gain, norm_shift, expand_weight, expand_bias, reduce_weight, cotangent
):
    channels, tile_rows, tile_cols = image.shape
    pixels = tile_rows * tile_cols
    all_channels = channels * lax.axis_size("ch")
    hid_local = reduce_weight.shape[0]
    half = KSIZE // 2
    padded = padded_2(image, (("row", 1), ("col", 2)), half).astype(jnp.float32)
    mixed = forward_taps(padded, depth_kernel, KSIZE, tile_rows, tile_cols)
    flat_cot = cotangent.reshape(channels, pixels)
    contract_first = (((0,), (0,)), ((), ()))
    contract_last = (((1,), (1,)), ((), ()))
    plain = (((1,), (0,)), ((), ()))
    centre = lax.psum(jnp.sum(mixed, axis=0), "ch") / all_channels
    diff = mixed - centre
    variance = lax.psum(jnp.sum(diff * diff, axis=0), "ch") / all_channels
    inverse = lax.rsqrt(variance + epsilon)
    normed = diff * inverse
    normal = (normed * norm_gain[:, None, None] + norm_shift[:, None, None]).astype(jnp.bfloat16)
    flat_normal = normal.reshape(channels, pixels)
    bias_local = lax.dynamic_slice_in_dim(expand_bias, lax.axis_index("ch") * hid_local, hid_local)
    full_normal = lax.all_gather(flat_normal, "ch", axis=0, tiled=True)
    hidden = product(expand_weight, full_normal, contract_first) + bias_local[:, None]
    value, slope = gelu_pair(hidden)
    active = value.astype(jnp.bfloat16)
    mlp_local = lax.psum_scatter(
        product(reduce_weight, active, contract_first), "ch", scatter_dimension=0, tiled=True
    )
    full_cot = lax.all_gather(flat_cot, "ch", axis=0, tiled=True)
    grad_act = product(reduce_weight, full_cot, plain)
    grad_hidden = (grad_act * slope).astype(jnp.bfloat16)
    grad_red = product(active, full_cot, contract_last)
    grad_exp = product(full_normal, grad_hidden, contract_last)
    grad_off = jnp.sum(grad_hidden.astype(jnp.float32), axis=1)
    grad_local = lax.psum_scatter(
        product(expand_weight, grad_hidden, plain).astype(jnp.bfloat16),
        "ch",
        scatter_dimension=0,
        tiled=True,
    ).astype(jnp.float32)
    grad_normal = grad_local.reshape(channels, tile_rows, tile_cols)
    grad_normed = grad_normal * norm_gain[:, None, None]
    plain_sum, cross_sum = lax.psum(
        (jnp.sum(grad_normed, axis=0), jnp.sum(grad_normed * normed, axis=0)), "ch"
    )
    grad_gain = jnp.sum(grad_normal * normed, axis=(1, 2))
    grad_shift = jnp.sum(grad_normal, axis=(1, 2))
    grad_mixed = inverse * (
        grad_normed - plain_sum / all_channels - normed * (cross_sum / all_channels)
    )
    result = (image.astype(jnp.float32) + mlp_local.reshape(channels, tile_rows, tile_cols)).astype(
        jnp.bfloat16
    )
    grad_pad = padded_2(grad_mixed.astype(jnp.bfloat16), (("row", 1), ("col", 2)), half).astype(
        grad_mixed.dtype
    )
    grad_image = (
        cotangent.astype(jnp.float32)
        + backward_taps(grad_pad, depth_kernel, KSIZE, tile_rows, tile_cols)
    ).astype(jnp.bfloat16)
    grad_kernel = kernel_grad(grad_mixed, padded, KSIZE, tile_rows, tile_cols)
    totals = lax.psum(
        (grad_kernel, grad_gain, grad_shift, grad_exp, grad_off, grad_red), ("row", "col")
    )
    pixels_all = pixels * lax.axis_size("row") * lax.axis_size("col")
    scale = float(pixels_all) ** (-0.5)
    return (
        result,
        grad_image,
        totals[0] * scale,
        totals[1] * scale,
        totals[2] * scale,
        totals[3] * scale,
        totals[4] * scale,
        totals[5] * scale,
    )


def solution(mesh):
    in_specs = (
        P("ch", "row", "col"),
        P("ch", None),
        P("ch"),
        P("ch"),
        P(None, "ch"),
        P(),
        P("ch", None),
        P("ch", "row", "col"),
    )
    out_specs = (
        P("ch", "row", "col"),
        P("ch", "row", "col"),
        P("ch", None),
        P("ch"),
        P("ch"),
        P(None, "ch"),
        P("ch"),
        P("ch", None),
    )
    return jax.shard_map(body, mesh=mesh, in_specs=in_specs, out_specs=out_specs, check_vma=False)
```

profile of v0, /device:TPU:1, one launch (start us, length us, event | category | flops | bytes accessed | tf_op | source)
XLA Modules:
  0.0 1113.7 jit_solution(2712978404241594079)
XLA Ops:
  8.1 1.0 fusion.13
  9.0 4.6 collective-permute-start
  13.6 5.5 collective-permute-start.1
  20.3 2.8 collective-permute-start.2
  23.1 1.3 collective-permute-start.3
  24.4 10.6 all_gather.7
  36.5 57.9 %while.48 = (s32[]{:T(128)}, f32[64,4,128]{2,1,0:T(4,128)S(1)}, f32[64,49]{0,1:T(8,128)}, f32[64,10,134]{2,1,0:T(8,128)S(1)}, s32[]{:T(128)}, /*index=5*/s32[]{:T(128)}, s32[]{:T(128)}, s32[]{:T(128)}, s32[]{:T(128)}, s32[]{:T(128)}) while((s32[]{:T(128)}, f32[64,4,128]{2,1,0:T(4,128)S(1)}, f32[64,49]{0,1:T(8,128)}, ...), condition=%wide.region_1.2_spmd.clone, body=%wide.region_0.1_spmd.clone.sunk | while | flops 98325 | bytes 394290 | solution.py:61
  94.4 7.8 psum.70
  102.4 6.0 psum.71
  109.3 10.1 all_gather.6
  119.6 1.1 fusion.8
  123.7 1.0 copy.25
  124.7 346.0 %all-reduce.5.cloned.1.call-done = (f32[256,256]{1,0:T(8,128)}, f32[256,256]{1,0:T(8,128)}) async-done(((f32[256,256]{1,0:T(8,128)}, f32[256,256]{1,0:T(8,128)}), (f32[256,256]{1,0:T(8,128)}, f32[256,256]{1,0:T(8,128)})) %all-reduce.5.cloned.1.call-update) | async-done | bytes 524304 | tf_op jit(solution)/shard_map/psum | solution.py:155
  470.8 1.9 broadcast_multiply_fusion
  472.6 1.0 copy.28
  474.4 8.4 all-reduce.2
  482.9 50.7 %while.47 = (s32[]{:T(128)}, f32[64,49]{0,1:T(8,128)S(1)}, f32[64,10,134]{2,1,0:T(8,128)S(1)}, f32[64,4,128]{2,1,0:T(4,128)S(1)}, s32[]{:T(128)}, /*index=5*/s32...) while((s32[]{:T(128)}, f32[64,49]{0,1:T(8,128)S(1)}, f32[64,10,134]{2,1,0:T(8,128)S(1)}, ...), condition=%wide.region_16.17_spmd, body=%wide.region_14.16_spmd.sunk | while | flops 65492 | bytes 263208 | solution.py:90
  483.0 0.9 multiply_reduce_fusion.6
  484.0 0.9 multiply_reduce_fusion.6
  485.1 0.9 multiply_reduce_fusion.6
  489.2 0.9 multiply_reduce_fusion.6
  490.2 0.9 multiply_reduce_fusion.6
  491.3 0.9 multiply_reduce_fusion.6
  533.7 477.5 %all-reduce = (f32[64,49]{0,1:T(8,128)S(1)}, f32[64]{0:T(128)S(1)}, f32[64]{0:T(128)S(1)}, f32[256]{0:T(256)S(1)}) all-reduce(f32[64,49]{0,1:T(8,128)S(1)} %get-tuple-element.351, f32[64]{0:T(128)S(1)} %get-tuple-element.382, f32[64]{0:T(128)S(1)} %get-tuple-element.384, ...), channel_id=1, replica_groups=mesh['row'=8,'col'=16,'ch'=4] {'row','col'}, use_global_device_ids=true, to_apply=%region_17.18 | all-reduce | flops 3520 | bytes 28160 | tf_op jit(solution)/shard_map/psum | solution.py:155
  1012.4 1.9 collective-permute-start.4
  1014.3 19.1 %collective-permute-start.5 = (bf16[64,3,128]{2,1,0:T(4,128)(2,1)S(1)}, bf16[64,3,128]{2,1,0:T(4,128)(2,1)S(1)}, u32[]{:S(2)}, u32[]{:S(2)}) collective-permute-start(bf16[64,3,128]{2,1,0:T(4,128)(2,1)S(1)} %get-tuple-element.425), channel_id=1, source_target_pairs={{64,0},{128,64},{192,128},{256,192},{320,256},{384,320},{448,384},... | collective-permute-start | bytes 147464 | tf_op jit(solution)/shard_map/ppermute | solution.py:20
  1034.6 1.3 collective-permute-start.6
  1035.9 1.3 collective-permute-start.7
  1037.7 3.5 collective-permute-done.6
  1041.2 3.8 collective-permute-done.7
  1045.8 57.9 %while.49 = (s32[]{:T(128)}, f32[64,4,128]{2,1,0:T(4,128)S(1)}, f32[64,49]{0,1:T(8,128)}, f32[64,10,134]{2,1,0:T(8,128)S(1)}, s32[]{:T(128)}, /*index=5*/s32[]{:...) while((s32[]{:T(128)}, f32[64,4,128]{2,1,0:T(4,128)S(1)}, ...), condition=%wide.region_13.14_spmd.clone, body=%wide.region_12.13_spmd.clone.sunk | while | flops 98327 | bytes 394322 | solution.py:74
  1104.4 1.0 copy.26
  (350 shorter events, 165.8 us)
Async XLA Ops:
  8.0 112.7 %copy-start = (bf16[256,256]{1,0:T(8,128)(2,1)S(1)}, bf16[256,256]{1,0:T(8,128)(2,1)}, u32[]{:S(2)}) copy-start(bf16[256,256]{1,0:T(8,128)(2,1)} %param.20) | copy-start | bytes 393220
  8.0 11.1 copy-start.3
  8.0 462.7 %all-reduce.5.cloned.1.call-start = ((), (), s32[]{:S(2)}) async-start(), calls=%async_computation.4 | async-start | bytes 1048576 | tf_op jit(solution)/shard_map/psum | solution.py:155
  9.0 10.1 collective-permute-start
  13.6 6.3 collective-permute-start.1
  19.1 0.9 copy-start.1
  20.3 15.5 %collective-permute-start.2 = (bf16[64,10,3]{2,1,0:T(8,128)(2,1)S(1)}, bf16[64,10,3]{2,1,0:T(8,128)(2,1)S(1)}, u32[]{:S(2)}, u32[]{:S(2)}) collective-permute-start(bf16[64,10,3]{2,1,0:T(8,128)(2,1)S(1)} %get-tuple-element.422), channel_id=1, source_target_pairs={{0,4},{4,8},{8,12},{12,16},{16,20},{20,24},{24,28},{28,32},{32,36}... | collective-permute-start | bytes 11528 | tf_op jit(solution)/shard_map/ppermute | solution.py:19
  23.1 12.7 %collective-permute-start.3 = (bf16[64,10,3]{2,1,0:T(8,128)(2,1)S(1)}, bf16[64,10,3]{2,1,0:T(8,128)(2,1)S(1)}, u32[]{:S(2)}, u32[]{:S(2)}) collective-permute-start(bf16[64,10,3]{2,1,0:T(8,128)(2,1)S(1)} %get-tuple-element.423), channel_id=1, source_target_pairs={{4,0},{8,4},{12,8},{16,12},{20,16},{24,20},{28,24},{32,28},{36,32}... | collective-permute-start | bytes 11528 | tf_op jit(solution)/shard_map/ppermute | solution.py:20
  108.4 0.7 copy-start.4
  108.4 0.7 copy-start.5
  109.3 10.1 copy-start.2
  122.1 350.5 %reduce-scatter.9.cloned.1.call-start = ((), (), s32[]{:S(2)}) async-start(), calls=%async_computation.3 | async-start | bytes 327680
  123.3 981.1 %reduce-scatter.7.cloned.1.call-start = ((), (), s32[]{:S(2)}) async-start(), calls=%async_computation.2 | async-start | bytes 655360
  1012.4 21.6 %collective-permute-start.4 = (bf16[64,3,128]{2,1,0:T(4,128)(2,1)S(1)}, bf16[64,3,128]{2,1,0:T(4,128)(2,1)S(1)}, u32[]{:S(2)}, u32[]{:S(2)}) collective-permute-start(bf16[64,3,128]{2,1,0:T(4,128)(2,1)S(1)} %get-tuple-element.424), channel_id=1, source_target_pairs={{0,64},{64,128},{128,192},{192,256},{256,320},{320,384},{384,448},... | collective-permute-start | bytes 147464 | tf_op jit(solution)/shard_map/ppermute | solution.py:19
  1014.3 20.0 %collective-permute-start.5 = (bf16[64,3,128]{2,1,0:T(4,128)(2,1)S(1)}, bf16[64,3,128]{2,1,0:T(4,128)(2,1)S(1)}, u32[]{:S(2)}, u32[]{:S(2)}) collective-permute-start(bf16[64,3,128]{2,1,0:T(4,128)(2,1)S(1)} %get-tuple-element.425), channel_id=1, source_target_pairs={{64,0},{128,64},{192,128},{256,192},{320,256},{384,320},{448,384},... | collective-permute-start | bytes 147464 | tf_op jit(solution)/shard_map/ppermute | solution.py:20
  1034.6 6.7 collective-permute-start.6
  1035.9 9.2 collective-permute-start.7
Sparse Core Ops, SparseCore 0:
  122.3 348.4 all-reduce.4
Sparse Core Ops, SparseCore 1:
  125.4 38.8 reduce-scatter.8
  167.0 28.9 reduce-scatter.6
where the time goes:
time: 1120 us; the launch traced here: 1110 us
  blocking collectives  520 us (46%)
  waiting for transfers between devices  355 us (32%)
  other arithmetic  97.2 us (9%)
  local copies, waits for them, and re-layouts  76.4 us (7%)
  starting transfers between devices  37.9 us (3%)
  between operations  15.7 us (1%)
    psum x1, blocking collectives, body(): lax.psum((grad_kernel, grad_gain, grad_shift, grad_exp, grad_off, grad_re...  477 us
    psum x1, waiting for transfers between devices, body(): lax.psum((grad_kernel, grad_gain, grad_shift, grad_exp, grad_off, grad_re...  346 us
    mul x98, local copies, waits for them, and re-layouts, tap_window(): return weight[:, :, None] * window  68.2 us
    reduce_sum x49, other arithmetic, kernel_step(): column = jnp.sum(grad_mixed * window, axis=(1, 2))  46.4 us
    ppermute x4, starting transfers between devices, padded_2(): after = lax.ppermute(leading, axis, down)  27.1 us
  transfers between devices with their start and end apart: 11, of which 5 were waited for; matrix products, arithmetic and copies ran while one was open for 10% of the time, Pallas kernels for 0%

commit v1 on v0

--- a/solution.py
+++ b/solution.py
@@ -153,7 +153,7 @@
     ).astype(jnp.bfloat16)
     grad_kernel = kernel_grad(grad_mixed, padded, KSIZE, tile_rows, tile_cols)
     totals = lax.psum(
-        (grad_kernel, grad_gain, grad_shift, grad_exp, grad_off, grad_red), ("row", "col")
+        lax.psum((grad_kernel, grad_gain, grad_shift, grad_exp, grad_off, grad_red), "col"), "row"
     )
     pixels_all = pixels * lax.axis_size("row") * lax.axis_size("col")
     scale = float(pixels_all) ** (-0.5)

time: 1120 us -> 509 us (0.45)
  blocking collectives: 520 us -> 130 us
  waiting for transfers between devices: 355 us -> 150 us
  starting transfers between devices: 37.9 us -> 23.6 us
    psum x1, blocking collectives: 477 us -> 40.5 us  [body(): lax.psum((grad_kernel, grad_gain, grad_shift, grad_exp, grad_off, grad_re...]
    psum x1, waiting for transfers between devices: 346 us -> 140 us  [body(): lax.psum((grad_kernel, grad_gain, grad_shift, grad_exp, grad_off, grad_re...]
    psum x0 -> x1, blocking collectives: none -> 46.7 us  [body(): lax.psum(lax.psum((grad_kernel, grad_gain, grad_shift, grad_exp, grad_off...]
    ppermute x4, starting transfers between devices: 27.1 us -> 11.2 us  [padded_2(): after = lax.ppermute(leading, axis, down)]
  transfers between devices with their start and end apart: 11 -> 12, of which waited for: 5 -> 5; matrix products, arithmetic and copies ran while one was open for 10% -> 23% of each run, Pallas kernels for 0% -> 0%
where the time goes in v1:
time: 509 us; the launch traced here: 504 us
  waiting for transfers between devices  150 us (29%)
  blocking collectives  130 us (26%)
  other arithmetic  97.2 us (19%)
  local copies, waits for them, and re-layouts  76.4 us (15%)
  starting transfers between devices  23.6 us (5%)
  between operations  15.8 us (3%)
  loops' own time  8.1 us (2%)
    psum x1, waiting for transfers between devices, body(): lax.psum((grad_kernel, grad_gain, grad_shift, grad_exp, grad_off, grad_re...  140 us
    mul x98, local copies, waits for them, and re-layouts, tap_window(): return weight[:, :, None] * window  68.2 us
    psum x1, blocking collectives, body(): lax.psum(lax.psum((grad_kernel, grad_gain, grad_shift, grad_exp, grad_off...  46.7 us
    reduce_sum x49, other arithmetic, kernel_step(): column = jnp.sum(grad_mixed * window, axis=(1, 2))  46.4 us
    psum x1, blocking collectives, body(): lax.psum((grad_kernel, grad_gain, grad_shift, grad_exp, grad_off, grad_re...  40.5 us
    add x49, other arithmetic, backward_step(): accum + tap_window(padded, kernel, tap, first, second, tile_rows, tile_cols)  21.2 us
    add x49, other arithmetic, forward_step(): accum + tap_window(padded, kernel, tap, first, second, tile_rows, tile_cols)  21.2 us
    ppermute x4, starting transfers between devices, padded_2(): before = lax.ppermute(last, axis, up)  12.3 us
  transfers between devices with their start and end apart: 12, of which 5 were waited for; matrix products, arithmetic and copies ran while one was open for 23% of the time, Pallas kernels for 0%

profile of v1, /device:TPU:1, one launch (start us, length us, event | category | flops | bytes accessed | tf_op | source)
XLA Modules:
  0.0 504.4 jit_solution(5220785638814562400)
XLA Ops:
  8.1 1.0 fusion.13
  9.0 4.6 collective-permute-start
  13.6 5.5 %collective-permute-start.1 = (bf16[64,3,128]{2,1,0:T(4,128)(2,1)S(1)}, bf16[64,3,128]{2,1,0:T(4,128)(2,1)S(1)}, u32[]{:S(2)}, u32[]{:S(2)}) collective-permute-start(bf16[64,3,128]{2,1,0:T(4,128)(2,1)S(1)} %get-tuple-element.433), channel_id=1, source_target_pairs={{64,0},{128,64},{192,128},{256,192},{320,256},{384,320},{448,384},... | collective-permute-start | bytes 147464 | tf_op jit(solution)/shard_map/ppermute | solution.py:20
  20.3 2.8 collective-permute-start.2
  23.1 1.3 collective-permute-start.3
  24.4 10.6 %all_gather.7 = bf16[256,512]{1,0:T(8,128)(2,1)S(1)} all-gather(bf16[64,512]{1,0:T(8,128)(2,1)S(1)} %bitcast.43), channel_id=1, replica_groups=mesh['row'=8,'col'=16,'ch'=4] {'ch'}, dimensions={0}, use_global_device_ids=true | all-gather | bytes 327680 | tf_op jit(solution)/shard_map/all_gather | solution.py:122
  36.5 57.9 %while.48 = (s32[]{:T(128)}, f32[64,4,128]{2,1,0:T(4,128)S(1)}, f32[64,49]{0,1:T(8,128)}, f32[64,10,134]{2,1,0:T(8,128)S(1)}, s32[]{:T(128)}, /*index=5*/s32[]{:T(128)}, s32[]{:T(128)}, s32[]{:T(128)}, s32[]{:T(128)}, s32[]{:T(128)}) while((s32[]{:T(128)}, f32[64,4,128]{2,1,0:T(4,128)S(1)}, f32[64,49]{0,1:T(8,128)}, ...), condition=%wide.region_1.2_spmd.clone, body=%wide.region_0.1_spmd.clone.sunk | while | flops 98325 | bytes 394290 | solution.py:61
  94.4 7.8 %psum.112 = f32[4,128]{1,0:T(4,128)S(1)} all-reduce(f32[4,128]{1,0:T(4,128)S(1)} %reduce_sum.81), channel_id=1, replica_groups=mesh['row'=8,'col'=16,'ch'=4] {'ch'}, use_global_device_ids=true, to_apply=%region_3.4 | all-reduce | flops 512 | bytes 4096 | tf_op jit(solution)/shard_map/psum | solution.py:107
  102.4 6.0 %psum.113 = f32[4,128]{1,0:T(4,128)S(1)} all-reduce(f32[4,128]{1,0:T(4,128)S(1)} %multiply_reduce_fusion.4), channel_id=1, replica_groups=mesh['row'=8,'col'=16,'ch'=4] {'ch'}, use_global_device_ids=true, to_apply=%region_5.6 | all-reduce | flops 512 | bytes 4096 | tf_op jit(solution)/shard_map/psum | solution.py:109
  109.3 10.1 %all_gather.6 = bf16[256,512]{1,0:T(8,128)(2,1)S(1)} all-gather(bf16[64,512]{1,0:T(8,128)(2,1)S(1)} %bitcast.44), channel_id=1, replica_groups=mesh['row'=8,'col'=16,'ch'=4] {'ch'}, dimensions={0}, use_global_device_ids=true | all-gather | bytes 327680 | tf_op jit(solution)/shard_map/all_gather | solution.py:115
  119.6 1.1 fusion.8
  123.4 139.6 %all-reduce.8.cloned.1.call-done = (f32[256,256]{1,0:T(8,128)}, f32[256,256]{1,0:T(8,128)}) async-done(((f32[256,256]{1,0:T(8,128)}, f32[256,256]{1,0:T(8,128)}), (f32[256,256]{1,0:T(8,128)}, f32[256,256]{1,0:T(8,128)})) %all-reduce.8.cloned.1.call-update) | async-done | bytes 524304 | tf_op jit(solution)/shard_map/psum | solution.py:156
  263.4 1.0 copy.25
  264.4 1.0 copy.28
  266.2 8.4 %all-reduce.4 = (f32[4,128]{1,0:T(4,128)S(1)}, f32[4,128]{1,0:T(4,128)S(1)}) all-reduce(f32[4,128]{1,0:T(4,128)S(1)} %get-tuple-element.383, f32[4,128]{1,0:T(4,128)S(1)} %bitcast.48), channel_id=1, replica_groups=mesh['row'=8,'col'=16,'ch'=4] {'ch'}, use_global_device_ids=true, to_apply=%region_11.12 | all-reduce | flops 1024 | bytes 8192 | tf_op jit(solution)/shard_map/psum | solution.py:136
  274.8 50.7 %while.47 = (s32[]{:T(128)}, f32[64,49]{0,1:T(8,128)S(1)}, f32[64,10,134]{2,1,0:T(8,128)S(1)}, f32[64,4,128]{2,1,0:T(4,128)S(1)}, s32[]{:T(128)}, /*index=5*/s32...) while((s32[]{:T(128)}, f32[64,49]{0,1:T(8,128)S(1)}, f32[64,10,134]{2,1,0:T(8,128)S(1)}, ...), condition=%wide.region_16.17_spmd, body=%wide.region_14.16_spmd.sunk | while | flops 65492 | bytes 263208 | solution.py:90
  275.8 0.9 multiply_reduce_fusion.6
  276.9 0.9 multiply_reduce_fusion.6
  277.9 0.9 multiply_reduce_fusion.6
  283.1 0.9 multiply_reduce_fusion.6
  325.5 40.5 %all-reduce = (f32[64,49]{0,1:T(8,128)S(1)}, f32[64]{0:T(128)S(1)}, f32[64]{0:T(128)S(1)}, f32[256]{0:T(256)S(1)}) all-reduce(f32[64,49]{0,1:T(8,128)S(1)} %get-tuple-element.351, f32[64]{0:T(128)S(1)} %get-tuple-element.382, f32[64]{0:T(128)S(1)} %get-tuple-element.384, ...), channel_id=1, replica_groups=mesh['row'=8,'col'=16,'ch'=4] {'col'}, use_global_device_ids=true, to_apply=%region_17.18 | all-reduce | flops 3520 | bytes 28160 | tf_op jit(solution)/shard_map/psum | solution.py:156
  366.0 46.7 %all-reduce.2 = (f32[64,49]{0,1:T(8,128)S(1)}, f32[64]{0:T(128)S(1)}, f32[64]{0:T(128)S(1)}, f32[256]{0:T(256)S(1)}) all-reduce(f32[64,49]{0,1:T(8,128)S(1)} %get-tuple-element.410, f32[64]{0:T(128)S(1)} %get-tuple-element.411, f32[64]{0:T(128)S(1)} %get-tuple-element.412, ...), channel_id=1, replica_groups=mesh['row'=8,'col'=16,'ch'=4] {'row'}, use_global_device_ids=true, to_apply=%region_18.19 | all-reduce | flops 3520 | bytes 28160 | tf_op jit(solution)/shard_map/psum | solution.py:155
  413.9 3.6 collective-permute-start.4
  417.5 3.1 collective-permute-start.5
  421.2 1.9 collective-permute-done.5
  423.4 1.3 collective-permute-start.6
  424.7 1.3 collective-permute-start.7
  426.6 3.2 collective-permute-done.6
  429.8 4.1 collective-permute-done.7
  434.6 57.9 %while.49 = (s32[]{:T(128)}, f32[64,4,128]{2,1,0:T(4,128)S(1)}, f32[64,49]{0,1:T(8,128)}, f32[64,10,134]{2,1,0:T(8,128)S(1)}, s32[]{:T(128)}, /*index=5*/s32[]{:...) while((s32[]{:T(128)}, f32[64,4,128]{2,1,0:T(4,128)S(1)}, ...), condition=%wide.region_13.14_spmd.clone, body=%wide.region_12.13_spmd.clone.sunk | while | flops 98327 | bytes 394322 | solution.py:74
  493.2 1.9 broadcast_multiply_fusion
  495.1 1.0 copy.26
  (354 shorter events, 167.4 us)
Async XLA Ops:
  8.0 112.7 %copy-start = (bf16[256,256]{1,0:T(8,128)(2,1)S(1)}, bf16[256,256]{1,0:T(8,128)(2,1)}, u32[]{:S(2)}) copy-start(bf16[256,256]{1,0:T(8,128)(2,1)} %param.20) | copy-start | bytes 393220
  8.0 11.1 %copy-start.3 = (bf16[64,4,128]{2,1,0:T(4,128)(2,1)S(1)}, bf16[64,4,128]{2,1,0:T(4,128)(2,1)}, u32[]{:S(2)}) copy-start(bf16[64,4,128]{2,1,0:T(4,128)(2,1)} %param.21) | copy-start | bytes 196612
  8.0 254.9 %all-reduce.8.cloned.1.call-start = ((), (), s32[]{:S(2)}) async-start(), calls=%async_computation.4 | async-start | bytes 1048576 | tf_op jit(solution)/shard_map/psum | solution.py:156
  9.0 10.1 %collective-permute-start = (bf16[64,3,128]{2,1,0:T(4,128)(2,1)S(1)}, bf16[64,3,128]{2,1,0:T(4,128)(2,1)S(1)}, u32[]{:S(2)}, u32[]{:S(2)}) collective-permute-start(bf16[64,3,128]{2,1,0:T(4,128)(2,1)S(1)} %get-tuple-element.432), channel_id=1, source_target_pairs={{0,64},{64,128},{128,192},{192,256},{256,320},{320,384},{384,448},... | collective-permute-start | bytes 147464 | tf_op jit(solution)/shard_map/ppermute | solution.py:19
  13.6 6.3 %collective-permute-start.1 = (bf16[64,3,128]{2,1,0:T(4,128)(2,1)S(1)}, bf16[64,3,128]{2,1,0:T(4,128)(2,1)S(1)}, u32[]{:S(2)}, u32[]{:S(2)}) collective-permute-start(bf16[64,3,128]{2,1,0:T(4,128)(2,1)S(1)} %get-tuple-element.433), channel_id=1, source_target_pairs={{64,0},{128,64},{192,128},{256,192},{320,256},{384,320},{448,384},... | collective-permute-start | bytes 147464 | tf_op jit(solution)/shard_map/ppermute | solution.py:20
  19.1 0.9 copy-start.1
  20.3 15.5 %collective-permute-start.2 = (bf16[64,10,3]{2,1,0:T(8,128)(2,1)S(1)}, bf16[64,10,3]{2,1,0:T(8,128)(2,1)S(1)}, u32[]{:S(2)}, u32[]{:S(2)}) collective-permute-start(bf16[64,10,3]{2,1,0:T(8,128)(2,1)S(1)} %get-tuple-element.428), channel_id=1, source_target_pairs={{0,4},{4,8},{8,12},{12,16},{16,20},{20,24},{24,28},{28,32},{32,36}... | collective-permute-start | bytes 11528 | tf_op jit(solution)/shard_map/ppermute | solution.py:19
  23.1 12.7 %collective-permute-start.3 = (bf16[64,10,3]{2,1,0:T(8,128)(2,1)S(1)}, bf16[64,10,3]{2,1,0:T(8,128)(2,1)S(1)}, u32[]{:S(2)}, u32[]{:S(2)}) collective-permute-start(bf16[64,10,3]{2,1,0:T(8,128)(2,1)S(1)} %get-tuple-element.429), channel_id=1, source_target_pairs={{4,0},{8,4},{12,8},{16,12},{20,16},{24,20},{28,24},{32,28},{36,32}... | collective-permute-start | bytes 11528 | tf_op jit(solution)/shard_map/ppermute | solution.py:20
  108.4 0.7 copy-start.4
  108.4 0.7 copy-start.5
  109.3 10.1 %copy-start.2 = (bf16[256,256]{1,0:T(8,128)(2,1)S(1)}, bf16[256,256]{1,0:T(8,128)(2,1)}, u32[]{:S(2)}) copy-start(bf16[256,256]{1,0:T(8,128)(2,1)} %param.18) | copy-start | bytes 393220
  122.1 142.3 %reduce-scatter.9.cloned.1.call-start = ((), (), s32[]{:S(2)}) async-start(), calls=%async_computation.3 | async-start | bytes 327680
  123.3 369.9 %all-reduce.10.cloned.1.call-start = ((), (), s32[]{:S(2)}) async-start(), calls=%async_computation.5 | async-start | bytes 1048576 | tf_op jit(solution)/shard_map/psum | solution.py:155
  263.0 232.1 %reduce-scatter.7.cloned.1.call-start = ((), (), s32[]{:S(2)}) async-start(), calls=%async_computation.2 | async-start | bytes 655360
  413.9 7.3 %collective-permute-start.4 = (bf16[64,3,128]{2,1,0:T(4,128)(2,1)S(1)}, bf16[64,3,128]{2,1,0:T(4,128)(2,1)S(1)}, u32[]{:S(2)}, u32[]{:S(2)}) collective-permute-start(bf16[64,3,128]{2,1,0:T(4,128)(2,1)S(1)} %get-tuple-element.430), channel_id=1, source_target_pairs={{0,64},{64,128},{128,192},{192,256},{256,320},{320,384},{384,448},... | collective-permute-start | bytes 147464 | tf_op jit(solution)/shard_map/ppermute | solution.py:19
  417.5 5.6 %collective-permute-start.5 = (bf16[64,3,128]{2,1,0:T(4,128)(2,1)S(1)}, bf16[64,3,128]{2,1,0:T(4,128)(2,1)S(1)}, u32[]{:S(2)}, u32[]{:S(2)}) collective-permute-start(bf16[64,3,128]{2,1,0:T(4,128)(2,1)S(1)} %get-tuple-element.431), channel_id=1, source_target_pairs={{64,0},{128,64},{192,128},{256,192},{320,256},{384,320},{448,384},... | collective-permute-start | bytes 147464 | tf_op jit(solution)/shard_map/ppermute | solution.py:20
  423.4 6.4 %collective-permute-start.6 = (bf16[64,10,3]{2,1,0:T(8,128)(2,1)S(1)}, bf16[64,10,3]{2,1,0:T(8,128)(2,1)S(1)}, u32[]{:S(2)}, u32[]{:S(2)}) collective-permute-start(bf16[64,10,3]{2,1,0:T(8,128)(2,1)S(1)} %get-tuple-element.426), channel_id=1, source_target_pairs={{0,4},{4,8},{8,12},{12,16},{16,20},{20,24},{24,28},{28,32},{32,36}... | collective-permute-start | bytes 11528 | tf_op jit(solution)/shard_map/ppermute | solution.py:19
  424.7 9.2 %collective-permute-start.7 = (bf16[64,10,3]{2,1,0:T(8,128)(2,1)S(1)}, bf16[64,10,3]{2,1,0:T(8,128)(2,1)S(1)}, u32[]{:S(2)}, u32[]{:S(2)}) collective-permute-start(bf16[64,10,3]{2,1,0:T(8,128)(2,1)S(1)} %get-tuple-element.427), channel_id=1, source_target_pairs={{4,0},{8,4},{12,8},{16,12},{20,16},{24,20},{28,24},{32,28},{36,32}... | collective-permute-start | bytes 11528 | tf_op jit(solution)/shard_map/ppermute | solution.py:20
Sparse Core Ops, SparseCore 0:
  122.3 140.6 all-reduce.7
  265.4 81.5 all-reduce.9
Sparse Core Ops, SparseCore 1:
  126.0 38.7 reduce-scatter.8
  266.3 33.2 reduce-scatter.6
